TPU v7x, 32 devices: a whole 2x2x4 slice. The times are simulated.
32 devices in a mesh: fsdp: 16 (over z, y, core), seq: 2 (over x).
Axes of the slice: x: 2, y: 2, z: 4, core: 2. Of those that a mesh axis runs over, the one named last changes fastest.
Arguments:
- tokens: bfloat16 [16, 1024, 1024], P('fsdp', 'seq'), may hold values from -6 to 6
- condition: bfloat16 [16, 1024], P('fsdp'), may hold values from -6 to 6
- w_ada: bfloat16 [1024, 6144], P('fsdp'), may hold values from -0.1875 to 0.1875
- b_ada: bfloat16 [6144], P('fsdp'), may hold values from -3 to 3
- w_qkv: bfloat16 [1024, 3072], P('fsdp'), may hold values from -0.1875 to 0.1875
- b_qv: bfloat16 [2048], P('fsdp'), may hold values from -1.1953125 to 1.1953125
- w_proj: bfloat16 [1024, 1024], P('fsdp'), may hold values from -0.1875 to 0.1875
- b_proj: bfloat16 [1024], P('fsdp'), may hold values from -1.1953125 to 1.1953125
- w_fc1: bfloat16 [1024, 4096], P('fsdp'), may hold values from -0.1875 to 0.1875
- b_fc1: bfloat16 [4096], P('fsdp'), may hold values from -1.1953125 to 1.1953125
- w_fc2: bfloat16 [4096, 1024], P('fsdp'), may hold values from -0.09375 to 0.09375
- b_fc2: bfloat16 [1024], P('fsdp'), may hold values from -1.1953125 to 1.1953125
- cotangent: bfloat16 [16, 1024, 1024], P('fsdp', 'seq'), may hold values from -6 to 6
Outputs:
- out_tokens: bfloat16 [16, 1024, 1024], P('fsdp', 'seq')
- grad_tokens: float32 [16, 1024, 1024], P('fsdp', 'seq')
- grad_condition: float32 [16, 1024], P('fsdp')
- grad_w_ada: float32 [1024, 6144], P('fsdp')
- grad_b_ada: float32 [6144], P('fsdp')
- grad_w_qkv: float32 [1024, 3072], P('fsdp')
- grad_b_qv: float32 [2048], P('fsdp')
- grad_w_proj: float32 [1024, 1024], P('fsdp')
- grad_b_proj: float32 [1024], P('fsdp')
- grad_w_fc1: float32 [1024, 4096], P('fsdp')
- grad_b_fc1: float32 [4096], P('fsdp')
- grad_w_fc2: float32 [4096, 1024], P('fsdp')
- grad_b_fc2: float32 [1024], P('fsdp')
All inputs are finite; a program needn't handle non-finite values.
Results may differ from a plain program's by a relative error of at most 0.018.
The roundings to bfloat16 on the way count: a program that leaves them out, or rounds other values in their place, can miss the bound.
Values may be sent and summed in bfloat16 or wider, within the bound.
A program may use at most 256 MiB of HBM per device.

v0:
```python
from functools import partial
import jax
import jax.numpy as jnp
from jax import lax
from jax.sharding import PartitionSpec as P

HD = 64
norm_eps = 1e-06
block_rows = 512


def layer_norm(values):
    center = values - jnp.mean(values, axis=-1, keepdims=True)
    rscale = lax.rsqrt(jnp.mean(center * center, axis=-1, keepdims=True) + norm_eps)
    return (center * rscale, rscale)


def norm_back(upstream, normed, rscale):
    mean_up = jnp.mean(upstream, axis=-1, keepdims=True)
    mean_cross = jnp.mean(upstream * normed, axis=-1, keepdims=True)
    return rscale * (upstream - mean_up - normed * mean_cross)


def attend_forward(queries, keys_all, values_all):
    seq_len = keys_all.shape[1]
    rows = min(block_rows, seq_len)
    score_scale = queries.shape[-1] ** (-0.5)
    outputs = []
    totals = []
    for offset in range(0, seq_len, rows):
        q_block = queries[:, offset : offset + rows]
        raw_scores = jnp.einsum(
            "bqhd,bkhd->bhqk", q_block, keys_all, preferred_element_type=jnp.float32
        )
        scores = raw_scores * score_scale
        row_max = jnp.max(scores, axis=-1, keepdims=True)
        shifted = jnp.exp(scores - row_max)
        row_total = jnp.sum(shifted, axis=-1, keepdims=True)
        attn_prob = (shifted / row_total).astype(jnp.bfloat16)
        block_out = jnp.einsum(
            "bhqk,bkhd->bqhd", attn_prob, values_all, preferred_element_type=jnp.float32
        )
        outputs.append(block_out.astype(jnp.bfloat16))
        totals.append(row_max + jnp.log(row_total))
    return (jnp.concatenate(outputs, axis=1), jnp.concatenate(totals, axis=2))


def attend_backward(queries, keys_all, values_all, log_total, d_out):
    seq_len = keys_all.shape[1]
    rows = min(block_rows, seq_len)
    score_scale = queries.shape[-1] ** (-0.5)
    grad_keys = jnp.zeros(keys_all.shape, jnp.float32)
    grad_values = jnp.zeros(values_all.shape, jnp.float32)
    grad_queries = []
    for offset in range(0, seq_len, rows):
        q_block = queries[:, offset : offset + rows]
        d_block = d_out[:, offset : offset + rows]
        raw_scores = jnp.einsum(
            "bqhd,bkhd->bhqk", q_block, keys_all, preferred_element_type=jnp.float32
        )
        attn_prob = jnp.exp(raw_scores * score_scale - log_total[:, :, offset : offset + rows])
        grad_values = grad_values + jnp.einsum(
            "bhqk,bqhd->bkhd",
            attn_prob.astype(jnp.bfloat16),
            d_block,
            preferred_element_type=jnp.float32,
        )
        d_prob = jnp.einsum(
            "bqhd,bkhd->bhqk", d_block, values_all, preferred_element_type=jnp.float32
        )
        center = jnp.sum(attn_prob * d_prob, axis=-1, keepdims=True)
        d_raw = (attn_prob * (d_prob - center) * score_scale).astype(jnp.bfloat16)
        grad_queries.append(
            jnp.einsum("bhqk,bkhd->bqhd", d_raw, keys_all, preferred_element_type=jnp.float32)
        )
        grad_keys = grad_keys + jnp.einsum(
            "bhqk,bqhd->bkhd", d_raw, q_block, preferred_element_type=jnp.float32
        )
    grad_q = jnp.concatenate(grad_queries, axis=1).astype(jnp.bfloat16)
    return (grad_q, grad_keys.astype(jnp.bfloat16), grad_values.astype(jnp.bfloat16))


def on_device(
    tokens,
    condition,
    w_ada,
    b_ada,
    w_qkv,
    b_qv,
    w_proj,
    b_proj,
    w_fc1,
    b_fc1,
    w_fc2,
    b_fc2,
    cotangent,
):
    latents, local_len, model_width = tokens.shape
    groups = lax.axis_size("seq")
    head_dim = HD
    group_width = model_width // groups
    per_group = group_width // head_dim
    ada_w, ada_b, qkv_w, qv_b, proj_w, proj_b, fc1_w, fc1_b, fc2_w, fc2_b = (
        lax.all_gather(w_ada, "fsdp", axis=0, tiled=True),
        lax.all_gather(b_ada, "fsdp", axis=0, tiled=True),
        lax.all_gather(w_qkv, "fsdp", axis=0, tiled=True),
        lax.all_gather(b_qv, "fsdp", axis=0, tiled=True),
        lax.all_gather(w_proj, "fsdp", axis=0, tiled=True),
        lax.all_gather(b_proj, "fsdp", axis=0, tiled=True),
        lax.all_gather(w_fc1, "fsdp", axis=0, tiled=True),
        lax.all_gather(b_fc1, "fsdp", axis=0, tiled=True),
        lax.all_gather(w_fc2, "fsdp", axis=0, tiled=True),
        lax.all_gather(b_fc2, "fsdp", axis=0, tiled=True),
    )
    tokens_f = tokens.astype(jnp.float32)
    lifted, silu_back = jax.vjp(jax.nn.silu, condition.astype(jnp.float32))
    lifted_b = lifted.astype(jnp.bfloat16)
    modulation = jnp.dot(lifted_b, ada_w, preferred_element_type=jnp.float32) + ada_b.astype(
        jnp.float32
    )
    shift_one, scale_one, gate_one, shift_two, scale_two, gate_two = jnp.split(
        modulation[:, None, :], 6, axis=-1
    )
    normed_one, rscale_one = layer_norm(tokens_f)
    hidden_one = (normed_one * (1.0 + scale_one) + shift_one).astype(jnp.bfloat16)
    qkv_bias = jnp.concatenate(
        [qv_b[:model_width], jnp.zeros((model_width,), jnp.bfloat16), qv_b[model_width:]]
    ).astype(jnp.float32)
    qkv_tok = (jnp.dot(hidden_one, qkv_w, preferred_element_type=jnp.float32) + qkv_bias).astype(
        jnp.bfloat16
    )
    spread = lax.all_to_all(
        qkv_tok.reshape(latents, local_len, 3, groups, group_width),
        "seq",
        split_axis=3,
        concat_axis=1,
        tiled=True,
    )
    seq_len = spread.shape[1]
    queries = spread[:, :, 0, 0].reshape(latents, seq_len, per_group, head_dim)
    keys_all = spread[:, :, 1, 0].reshape(latents, seq_len, per_group, head_dim)
    values_all = spread[:, :, 2, 0].reshape(latents, seq_len, per_group, head_dim)
    attn_out, log_total = attend_forward(queries, keys_all, values_all)
    returned = lax.all_to_all(
        attn_out.reshape(latents, seq_len, 1, group_width),
        "seq",
        split_axis=1,
        concat_axis=2,
        tiled=True,
    )
    attn_tok = returned.reshape(latents, local_len, model_width)
    branch = jnp.dot(attn_tok, proj_w, preferred_element_type=jnp.float32) + proj_b.astype(
        jnp.float32
    )
    middle = tokens_f + gate_one * branch
    normed_two, rscale_two = layer_norm(middle)
    hidden_two = (normed_two * (1.0 + scale_two) + shift_two).astype(jnp.bfloat16)
    pre_act = jnp.dot(hidden_two, fc1_w, preferred_element_type=jnp.float32) + fc1_b.astype(
        jnp.float32
    )
    act_f, gelu_back = jax.vjp(partial(jax.nn.gelu, approximate=True), pre_act)
    act_b = act_f.astype(jnp.bfloat16)
    mlp_out = jnp.dot(act_b, fc2_w, preferred_element_type=jnp.float32) + fc2_b.astype(jnp.float32)
    result = (middle + gate_two * mlp_out).astype(jnp.bfloat16)
    grad_out = cotangent.astype(jnp.float32)
    d_gate_two = jnp.sum(grad_out * mlp_out, axis=1)
    d_mlp = (grad_out * gate_two).astype(jnp.bfloat16)
    grad_fc2 = jnp.einsum("btf,btd->fd", act_b, d_mlp, preferred_element_type=jnp.float32)
    bias_fc2 = jnp.sum(d_mlp, axis=(0, 1), dtype=jnp.float32)
    d_act = jnp.einsum("btd,fd->btf", d_mlp, fc2_w, preferred_element_type=jnp.float32)
    d_pre = gelu_back(d_act)[0].astype(jnp.bfloat16)
    grad_fc1 = jnp.einsum("btd,btf->df", hidden_two, d_pre, preferred_element_type=jnp.float32)
    bias_fc1 = jnp.sum(d_pre, axis=(0, 1), dtype=jnp.float32)
    d_hidden_two = jnp.einsum("btf,df->btd", d_pre, fc1_w, preferred_element_type=jnp.float32)
    d_shift_two = jnp.sum(d_hidden_two, axis=1)
    d_scale_two = jnp.sum(d_hidden_two * normed_two, axis=1)
    d_middle = grad_out + norm_back(d_hidden_two * (1.0 + scale_two), normed_two, rscale_two)
    d_gate_one = jnp.sum(d_middle * branch, axis=1)
    d_branch = (d_middle * gate_one).astype(jnp.bfloat16)
    grad_proj = jnp.einsum("btk,btd->kd", attn_tok, d_branch, preferred_element_type=jnp.float32)
    bias_proj = jnp.sum(d_branch, axis=(0, 1), dtype=jnp.float32)
    d_attn = jnp.einsum("btd,kd->btk", d_branch, proj_w, preferred_element_type=jnp.float32).astype(
        jnp.bfloat16
    )
    d_heads = lax.all_to_all(
        d_attn.reshape(latents, local_len, groups, group_width),
        "seq",
        split_axis=2,
        concat_axis=1,
        tiled=True,
    )
    d_heads = d_heads.reshape(latents, seq_len, per_group, head_dim)
    grad_q, grad_k, grad_v = attend_backward(queries, keys_all, values_all, log_total, d_heads)
    d_spread = jnp.stack([grad_q, grad_k, grad_v], axis=2).reshape(
        latents, seq_len, 3, 1, group_width
    )
    d_qkv = lax.all_to_all(d_spread, "seq", split_axis=1, concat_axis=3, tiled=True).reshape(
        latents, local_len, 3 * model_width
    )
    grad_qkv = jnp.einsum("btd,bte->de", hidden_one, d_qkv, preferred_element_type=jnp.float32)
    column_sums = jnp.sum(d_qkv, axis=(0, 1), dtype=jnp.float32)
    bias_qv = jnp.concatenate([column_sums[:model_width], column_sums[2 * model_width :]])
    d_hidden_one = jnp.einsum("bte,de->btd", d_qkv, qkv_w, preferred_element_type=jnp.float32)
    d_shift_one = jnp.sum(d_hidden_one, axis=1)
    d_scale_one = jnp.sum(d_hidden_one * normed_one, axis=1)
    grad_input = d_middle + norm_back(d_hidden_one * (1.0 + scale_one), normed_one, rscale_one)
    d_partial = jnp.concatenate(
        [d_shift_one, d_scale_one, d_gate_one, d_shift_two, d_scale_two, d_gate_two], axis=-1
    )
    d_modulation = lax.psum(d_partial, "seq").astype(jnp.bfloat16)
    d_lifted = jnp.einsum("be,ce->bc", d_modulation, ada_w, preferred_element_type=jnp.float32)
    grad_condition = silu_back(d_lifted)[0]
    grad_ada = jnp.einsum("bc,be->ce", lifted_b, d_modulation, preferred_element_type=jnp.float32)
    bias_ada = jnp.sum(d_modulation, axis=0, dtype=jnp.float32)
    total_ada, total_bada = (
        lax.psum_scatter(
            grad_ada.astype(jnp.bfloat16), "fsdp", scatter_dimension=0, tiled=True
        ).astype(jnp.float32),
        lax.psum_scatter(
            bias_ada.astype(jnp.bfloat16), "fsdp", scatter_dimension=0, tiled=True
        ).astype(jnp.float32),
    )
    shard_qkv, shard_bqv, shard_proj, shard_bproj, shard_fc1, shard_bfc1, shard_fc2, shard_bfc2 = (
        lax.psum_scatter(grad_qkv, "fsdp", scatter_dimension=0, tiled=True),
        lax.psum_scatter(bias_qv, "fsdp", scatter_dimension=0, tiled=True),
        lax.psum_scatter(grad_proj, "fsdp", scatter_dimension=0, tiled=True),
        lax.psum_scatter(bias_proj, "fsdp", scatter_dimension=0, tiled=True),
        lax.psum_scatter(grad_fc1, "fsdp", scatter_dimension=0, tiled=True),
        lax.psum_scatter(bias_fc1, "fsdp", scatter_dimension=0, tiled=True),
        lax.psum_scatter(grad_fc2, "fsdp", scatter_dimension=0, tiled=True),
        lax.psum_scatter(bias_fc2, "fsdp", scatter_dimension=0, tiled=True),
    )
    total_qkv, total_bqv, total_proj, total_bproj, total_fc1, total_bfc1, total_fc2, total_bfc2 = (
        lax.psum(
            (
                shard_qkv,
                shard_bqv,
                shard_proj,
                shard_bproj,
                shard_fc1,
                shard_bfc1,
                shard_fc2,
                shard_bfc2,
            ),
            "seq",
        )
    )
    return (
        result,
        grad_input,
        grad_condition,
        total_ada,
        total_bada,
        total_qkv,
        total_bqv,
        total_proj,
        total_bproj,
        total_fc1,
        total_bfc1,
        total_fc2,
        total_bfc2,
    )


def solution(mesh):
    return jax.shard_map(
        on_device,
        mesh=mesh,
        in_specs=(
            P("fsdp", "seq", None),
            P("fsdp", None),
            P("fsdp", None),
            P("fsdp"),
            P("fsdp", None),
            P("fsdp"),
            P("fsdp", None),
            P("fsdp"),
            P("fsdp", None),
            P("fsdp"),
            P("fsdp", None),
            P("fsdp"),
            P("fsdp", "seq", None),
        ),
        out_specs=(
            P("fsdp", "seq", None),
            P("fsdp", "seq", None),
            P("fsdp", None),
            P("fsdp", None),
            P("fsdp"),
            P("fsdp", None),
            P("fsdp"),
            P("fsdp", None),
            P("fsdp"),
            P("fsdp", None),
            P("fsdp"),
            P("fsdp", None),
            P("fsdp"),
        ),
        check_vma=False,
    )
```

profile of v0, /device:TPU:0, one launch (start us, length us, event | category | flops | bytes accessed | tf_op | source)
XLA Modules:
  0.0 1429.1 jit_solution(12914743900525769951)
XLA Ops:
  12.0 23.8 %all-gather.1 = bf16[16,1,128]{2,1,0:T(2,128)(2,1)S(1)} all-gather(bf16[1,1,128]{2,1,0:T(2,128)(2,1)} %bitcast.251), channel_id=1, replica_groups=mesh['fsdp'=16,'seq'=2] {'fsdp'}, dimensions={0}, use_global_device_ids=true | all-gather | bytes 4352 | tf_op jit(solution)/shard_map/all_gather | solution.py:107
  36.5 18.1 %all-gather = bf16[16,1,384]{2,1,0:T(2,128)(2,1)S(1)} all-gather(bf16[1,1,384]{2,1,0:T(2,128)(2,1)S(1)} %reshape.506), channel_id=1, replica_groups=mesh['fsdp'=16,'seq'=2] {'fsdp'}, dimensions={0}, use_global_device_ids=true | all-gather | bytes 13056 | tf_op jit(solution)/shard_map/all_gather | solution.py:105
  56.7 56.9 %all-gather.9.cloned.1.call-done = bf16[1024,6144]{1,0:T(8,128)(2,1)} async-done(((bf16[64,6144]{1,0:T(8,128)(2,1)}), bf16[1024,6144]{1,0:T(8,128)(2,1)}) %all-gather.9.cloned.1.call-update) | async-done | bytes 12582928 | tf_op jit(solution)/shard_map/all_gather | solution.py:104
  113.6 6.3 fusion.96
  120.0 55.6 %all-gather.11.cloned.1.call-done = bf16[1024,3072]{1,0:T(8,128)(2,1)} async-done(((bf16[64,3072]{1,0:T(8,128)(2,1)}), bf16[1024,3072]{1,0:T(8,128)(2,1)}) %all-gather.11.cloned.1.call-update) | async-done | bytes 6291472 | tf_op jit(solution)/shard_map/all_gather | solution.py:106
  175.6 7.8 add_convert_fusion
  183.4 7.1 reshape.484
  191.0 39.7 %all_to_all.63 = bf16[1,512,3,2,512]{4,1,2,0,3:T(8,128)(2,1)S(1)} all-to-all(bf16[1,512,3,2,512]{4,1,2,0,3:T(8,128)(2,1)S(1)} %copy.46), channel_id=1, replica_groups=mesh['fsdp'=16,'seq'=2] {'seq'}, dimensions={3} | all-to-all | bytes 6291456 | tf_op jit(solution)/shard_map/all_to_all | solution.py:132
  237.3 8.6 multiply_reduce_fusion.3
  249.4 5.6 copy-done.1
  262.9 7.8 fusion.72
  275.9 9.0 reduce.38
  287.5 4.5 all-to-all-start.1
  293.8 30.7 %all-reduce.10 = (bf16[1024]{0:T(1024)(128)(2,1)S(1)}, bf16[1024]{0:T(1024)(128)(2,1)S(1)}) all-reduce(bf16[1024]{0:T(1024)(128)(2,1)S(1)} %dynamic-update-slice, bf16[1024]{0:T(1024)(128)(2,1)S(1)} %dynamic-update-slice.1), channel_id=1, replica_groups=mesh['fsdp'=16,'seq'=2] {'fsdp'}, use_global_device_ids=true, to_apply=%add | all-reduce | flops 2048 | bytes 8192
  324.5 17.6 %all-gather.2 = bf16[16,1,256]{2,1,0:T(2,128)(2,1)S(1)} all-gather(bf16[1,1,256]{2,1,0:T(2,128)(2,1)S(1)} %reshape.510), channel_id=1, replica_groups=mesh['fsdp'=16,'seq'=2] {'fsdp'}, dimensions={0}, use_global_device_ids=true | all-gather | bytes 8704 | tf_op jit(solution)/shard_map/all_gather | solution.py:111
  350.3 4.6 fusion.127
  356.6 12.0 fusion.122
  368.6 13.9 convert_reduce_fusion
  382.5 9.8 fusion.55
  393.1 10.4 convert_reduce_fusion.3
  413.4 4.9 fusion.76
  418.4 9.5 all-to-all-done.2
  432.2 8.2 fusion.29
  440.4 8.7 add_convert_fusion.1
  449.1 5.9 copy.58
  455.0 8.1 fusion.90
  463.1 37.1 %fusion.64 = bf16[8,64,512]{2,1,0:T(8,128)(2,1)} fusion(bf16[1024,8,64]{0,2,1:T(8,128)(2,1)S(1)} %bitcast.199, f32[8,512,1024]{2,1,0:T(8,128)} %fusion.90, f32[8,512]{1,0:T(8,128)S(1)} %log_add_fusion, f32[8,512,1024]{2,1,0:T(8,128)} %copy-done), kind=kOutput, calls=%fused_computation.90 | convolution fusion | flops 574886912 | bytes 35143680 | tf_op jit(solution)/shard_map/bhqk,bkhd->bqhd/dot_general | solution.py:74
  503.7 8.1 fusion.89
  511.8 36.6 %fusion.67 = bf16[8,64,512]{2,1,0:T(8,128)(2,1)S(1)} fusion(bf16[1024,8,64]{0,2,1:T(8,128)(2,1)S(1)} %bitcast.200, f32[8,512,1024]{2,1,0:T(8,128)} %fusion.89, f32[8,512]{1,0:T(8,128)S(1)} %log_add_fusion.1, f32[8,512,1024]{2,1,0:T(8,128)} %get-tuple-element.67), kind=kOutput, calls=%fused_computation.91 | convolution fusion | flops 574886912 | bytes 35143680 | tf_op jit(solution)/shard_map/bhqk,bkhd->bqhd/dot_general | solution.py:74
  550.4 30.7 %fusion.11 = f32[8,64,1024]{2,1,0:T(8,128)} fusion(f32[8,512,1024]{2,1,0:T(8,128)} %fusion.89, f32[8,512,1024]{2,1,0:T(8,128)} %get-tuple-element.67, f32[8,512]{1,0:T(8,128)S(1)} %log_add_fusion.1, bf16[1,1024,8,64]{1,3,2,0:T(8,128)(2,1)S(1)} %bitcast.210), kind=kOutput, calls=%fused_computation.21 | convolution fusion | flops 574624768 | bytes 69763072 | tf_op jit(solution)/shard_map/bhqk,bqhd->bkhd/dot_general | solution.py:76
  581.1 31.5 %add_convert_fusion.2 = bf16[8,64,1024]{2,1,0:T(8,128)(2,1)} fusion(f32[8,64,1024]{2,1,0:T(8,128)} %fusion.11, f32[8,512,1024]{2,1,0:T(8,128)} %fusion.90, f32[8,512]{1,0:T(8,128)S(1)} %log_add_fusion, f32[8,512,1024]{2,1,0:T(8,128)} %copy-done, bf16[1,1024,8,64]{1,3,2,0:T(8,128)(2,1)} %bitcast.208), kind=kOutput, calls=%fused_computation.82 | convolution fusion | flops 575673344 | bytes 70811648 | tf_op jit(solution)/shard_map/bhqk,bqhd->bkhd/dot_general | solution.py:76
  612.6 5.9 copy.57
  618.5 8.6 pad_maximum_fusion
  627.1 50.3 %all_to_all.64 = bf16[1,1024,3,1,512]{4,2,3,0,1:T(4,128)(2,1)S(1)} all-to-all(bf16[1,1024,3,1,512]{4,2,3,0,1:T(4,128)(2,1)S(1)} %pad_maximum_fusion), channel_id=1, replica_groups=mesh['fsdp'=16,'seq'=2] {'seq'}, dimensions={1} | all-to-all | bytes 6291456 | tf_op jit(solution)/shard_map/all_to_all | solution.py:197
  681.1 10.5 fusion.117
  691.7 18.5 %fusion.79 = f32[4096,1024]{1,0:T(8,128)} fusion(bf16[1,512,1024]{2,1,0:T(8,128)(2,1)} %param.25, f32[1024]{0:T(1024)S(1)} %bitcast.243, f32[512,4096]{1,0:T(8,128)} %fusion.122, f32[4096]{0:T(1024)S(1)} %bitcast.236), kind=kOutput, calls=%fused_computation.102 | convolution fusion | flops 4317511680 | bytes 26234880 | tf_op jit(solution)/shard_map/btf,btd->fd/dot_general | solution.py:168
  710.8 15.0 %fusion.120 = f32[1024,4096]{1,0:T(8,128)} fusion(bf16[512,4096]{1,0:T(8,128)(2,1)} %copy-done.37, f32[1,512,1024]{2,1,0:T(8,128)} %copy-done.9, f32[1024]{0:T(1024)S(1)} %bitcast.240, f32[1024]{0:T(1024)S(1)} %bitcast.230, f32[512]{0:T(512)S(1)} %add_rsqrt_fusion, f32[512]{0:T(512)S(1)} %broadcast_multiply_fusion.4), kind=kOutput, calls=%fused_computation.165 | convolution fusion | flops 4297588736 | bytes 23080960 | tf_op jit(solution)/shard_map/btd,btf->df/dot_general | solution.py:172
  728.3 61.3 %all-reduce.7 = (f32[2048]{0:T(1024)S(1)}, f32[1024]{0:T(1024)S(1)}, f32[4096]{0:T(1024)S(1)}, f32[1024]{0:T(1024)S(1)}) all-reduce(f32[2048]{0:T(1024)S(1)} %pad_maximum_fusion.2, f32[1024]{0:T(1024)S(1)} %get-tuple-element.47, f32[4096]{0:T(1024)S(1)} %copy-done.21, ...), channel_id=5, replica_groups=mesh['fsdp'=16,'seq'=2] {'fsdp'}, use_global_device_ids=true, to_apply=%region_26.27.clone | all-reduce | flops 8192 | bytes 65536
  789.9 8.1 fusion.51
  800.8 9.9 all-reduce.8
  810.8 7.4 multiply_convert_fusion
  818.3 8.7 reduce-scatter.8.cloned.1.call-done
  827.0 180.7 %reduce-scatter.14.cloned.1.call-done = f32[256,1024]{1,0:T(8,128)} async-done(((f32[4096,1024]{1,0:T(8,128)}), f32[256,1024]{1,0:T(8,128)}) %reduce-scatter.14.cloned.1.call-update) | async-done | bytes 1048592 | tf_op jit(solution)/shard_map/reduce_scatter | solution.py:230
  1007.7 180.6 %reduce-scatter.12.cloned.1.call-done = f32[64,4096]{1,0:T(8,128)} async-done(((f32[1024,4096]{1,0:T(8,128)}), f32[64,4096]{1,0:T(8,128)}) %reduce-scatter.12.cloned.1.call-update) | async-done | bytes 1048592 | tf_op jit(solution)/shard_map/reduce_scatter | solution.py:228
  1188.9 61.3 %all-reduce.2 = bf16[6144]{0:T(1024)(128)(2,1)S(1)} all-reduce(bf16[6144]{0:T(1024)(128)(2,1)S(1)} %convert_reduce_fusion.5), channel_id=3, replica_groups=mesh['fsdp'=16,'seq'=2] {'fsdp'}, use_global_device_ids=true, to_apply=%region_22.23.clone | all-reduce | flops 6144 | bytes 24576
  1250.8 8.7 fusion.95
  1259.5 67.0 %reduce-scatter.6.cloned.1.call-done = bf16[64,6144]{1,0:T(8,128)(2,1)} async-done(((bf16[1024,6144]{1,0:T(8,128)(2,1)}), bf16[64,6144]{1,0:T(8,128)(2,1)}) %reduce-scatter.6.cloned.1.call-update) | async-done | bytes 786448 | tf_op jit(solution)/shard_map/reduce_scatter | solution.py:216
  1328.8 85.2 %all-reduce.13.cloned.1.call-done = (f32[64,3072]{1,0:T(8,128)}, f32[64,1024]{1,0:T(8,128)}, f32[64,4096]{1,0:T(8,128)}, f32[256,1024]{1,0:T(8,128)}) async-done(((f32[64,3072]{1,0:T(8,128)}, f32[64,1024]{1,0:T(8,128)}, f32[64,4096]{1,0:T(8,128)}, f32[256,1024]{1,0:T(8,128)}), (f32[64,3072]{1,0:T(8,128)}, f32[64,1024]{1,0:T(8,128)}, f32[64,4096]{1,0:T(8,128)}, ...) | async-done | bytes 3145744 | tf_op jit(solution)/shard_map/psum | solution.py:234
  (187 shorter events, 84.7 us)
Async XLA Ops:
  7.2 106.4 %all-gather.9.cloned.1.call-start = ((), (), s32[]{:S(2)}) async-start(), calls=%async_computation.9 | async-start | bytes 13369344 | tf_op jit(solution)/shard_map/all_gather | solution.py:104
  7.9 167.6 %all-gather.11.cloned.1.call-start = ((), (), s32[]{:S(2)}) async-start(), calls=%async_computation.10 | async-start | bytes 6684672 | tf_op jit(solution)/shard_map/all_gather | solution.py:106
  8.7 341.7 %all-gather.13.cloned.1.call-start = ((), (), s32[]{:S(2)}) async-start(), calls=%async_computation.11 | async-start | bytes 2228224 | tf_op jit(solution)/shard_map/all_gather | solution.py:108
  9.4 347.2 %all-gather.15.cloned.1.call-start = ((), (), s32[]{:S(2)}) async-start(), calls=%async_computation.12 | async-start | bytes 8912896 | tf_op jit(solution)/shard_map/all_gather | solution.py:110
  10.0 358.7 %all-gather.17.cloned.1.call-start = ((), (), s32[]{:S(2)}) async-start(), calls=%async_computation.13 | async-start | bytes 8912896 | tf_op jit(solution)/shard_map/all_gather | solution.py:112
  54.7 120.8 %copy-start.16 = (f32[512]{0:T(512)}, f32[512]{0:T(512)S(1)}, u32[]{:S(2)}) copy-start(f32[512]{0:T(512)S(1)} %broadcast_multiply_fusion.5) | copy-start | bytes 6148
  56.7 118.9 %copy-start.22 = (f32[512]{0:T(512)}, f32[512]{0:T(512)S(1)}, u32[]{:S(2)}) copy-start(f32[512]{0:T(512)S(1)} %add_rsqrt_fusion.1) | copy-start | bytes 6148
  56.7 118.9 %copy-start.2 = (bf16[1,512,1024]{2,1,0:T(8,128)(2,1)S(1)}, bf16[1,512,1024]{2,1,0:T(8,128)(2,1)}, u32[]{:S(2)}) copy-start(bf16[1,512,1024]{2,1,0:T(8,128)(2,1)} %param.13) | copy-start | bytes 3145732
  119.9 55.6 %copy-start.14 = (f32[1,1,1024]{2,1,0:T(1,128)}, f32[1,1,1024]{2,1,0:T(1,128)S(1)}, u32[]{:S(2)}) copy-start(f32[1,1,1024]{2,1,0:T(1,128)S(1)} %get-tuple-element.56) | copy-start | bytes 12292
  120.0 55.6 %copy-start.26 = (f32[1,1,1024]{2,1,0:T(1,128)}, f32[1,1,1024]{2,1,0:T(1,128)S(1)}, u32[]{:S(2)}) copy-start(f32[1,1,1024]{2,1,0:T(1,128)S(1)} %get-tuple-element.55) | copy-start | bytes 12292
  120.0 236.6 %copy-start.24 = (f32[1,1,1024]{2,1,0:T(1,128)}, f32[1,1,1024]{2,1,0:T(1,128)S(1)}, u32[]{:S(2)}) copy-start(f32[1,1,1024]{2,1,0:T(1,128)S(1)} %get-tuple-element.53) | copy-start | bytes 12292
  233.7 3.6 copy-start.7
  237.3 21.3 %copy-start = (f32[8,512,1024]{2,1,0:T(8,128)}, f32[8,512,1024]{2,1,0:T(8,128)S(1)}, u32[]{:S(2)}) copy-start(f32[8,512,1024]{2,1,0:T(8,128)S(1)} %get-tuple-element.65) | copy-start | bytes 50331652
  245.9 9.1 copy-start.1
  270.8 21.2 %copy-start.33 = (bf16[256]{0:T(256)(128)(2,1)S(1)}, bf16[256]{0:T(256)(128)(2,1)}, u32[]{:S(2)}) copy-start(bf16[256]{0:T(256)(128)(2,1)} %param.22) | copy-start | bytes 1540
  270.8 21.3 %copy-start.29 = (u32[32]{0:T(128)S(1)}, u32[32]{0:T(128)}, u32[]{:S(2)}) copy-start(u32[32]{0:T(128)} %constant.40) | copy-start | bytes 388
  270.8 22.5 %copy-start.34 = (bf16[64]{0:T(256)(128)(2,1)S(1)}, bf16[64]{0:T(256)(128)(2,1)}, u32[]{:S(2)}) copy-start(bf16[64]{0:T(256)(128)(2,1)} %param.24) | copy-start | bytes 388
  270.8 22.8 %copy-start.35 = (bf16[64]{0:T(256)(128)(2,1)S(1)}, bf16[64]{0:T(256)(128)(2,1)}, u32[]{:S(2)}) copy-start(bf16[64]{0:T(256)(128)(2,1)} %param.20) | copy-start | bytes 388
  275.3 75.0 %copy-start.3 = (bf16[1,512,1024]{2,1,0:T(8,128)(2,1)S(1)}, bf16[1,512,1024]{2,1,0:T(8,128)(2,1)}, u32[]{:S(2)}) copy-start(bf16[1,512,1024]{2,1,0:T(8,128)(2,1)} %param.13) | copy-start | bytes 3145732
  287.5 54.6 %all-to-all-start.1 = ((bf16[2,2,131072]{2,1,0:T(2,128)(2,1)}), bf16[2,2,131072]{2,1,0:T(2,128)(2,1)}, u32[]{:S(2)}, u32[]{:S(2)}) async-start(bf16[2,2,131072]{2,1,0:T(2,128)(2,1)} %reshape.533), calls=%async_computation.1 | async-start | bytes 2097152 | tf_op jit(solution)/shard_map/all_to_all | solution.py:144
  324.5 30.5 %copy-start.18 = (f32[1024]{0:T(1024)}, f32[1024]{0:T(1024)S(1)}, u32[]{:S(2)}) copy-start(f32[1024]{0:T(1024)S(1)} %convert_element_type.179) | copy-start | bytes 12292
  356.6 12.0 copy-start.32
  368.6 13.9 copy-start.10
  382.5 9.8 copy-start.37
  382.5 10.6 copy-start.30
  393.1 11.4 copy-start.31
  409.8 18.1 %all-to-all-start.2 = ((bf16[1,512,2,512]{3,1,0,2:T(8,128)(2,1)}), bf16[1,512,2,512]{3,1,0,2:T(8,128)(2,1)S(1)}, u32[]{:S(2)}, u32[]{:S(2)}) async-start(bf16[1,512,2,512]{3,1,0,2:T(8,128)(2,1)} %copy.53), calls=%async_computation.2 | async-start | bytes 2097152 | tf_op jit(solution)/shard_map/all_to_all | solution.py:185
  413.3 404.9 %reduce-scatter.10.cloned.1.call-start = ((), (), s32[]{:S(2)}) async-start(), calls=%async_computation.16 | async-start | bytes 4456448 | tf_op jit(solution)/shard_map/reduce_scatter | solution.py:226
  418.4 408.6 %reduce-scatter.8.cloned.1.call-start = ((), (), s32[]{:S(2)}) async-start(), calls=%async_computation.15 | async-start | bytes 13369344 | tf_op jit(solution)/shard_map/reduce_scatter | solution.py:224
  511.8 38.6 %copy-start.8 = (bf16[1,1024,1,1,512]{1,4,3,2,0:T(8,128)(2,1)S(1)}, bf16[1,1024,1,1,512]{1,4,3,2,0:T(8,128)(2,1)}, u32[]{:S(2)}) copy-start(bf16[1,1024,1,1,512]{1,4,3,2,0:T(8,128)(2,1)} %copy.49) | copy-start | bytes 3145732
  581.1 37.5 %copy-start.5 = (bf16[1,1024,1,1,512]{4,2,3,0,1:T(2,128)(2,1)S(1)}, bf16[1,1024,1,1,512]{4,2,3,0,1:T(2,128)(2,1)}, u32[]{:S(2)}) copy-start(bf16[1,1024,1,1,512]{4,2,3,0,1:T(2,128)(2,1)} %copy.58) | copy-start | bytes 3145732
  581.1 37.5 %copy-start.6 = (bf16[1,512,1,1,512]{4,2,3,0,1:T(2,128)(2,1)S(1)}, bf16[1,512,1,1,512]{4,2,3,0,1:T(2,128)(2,1)}, u32[]{:S(2)}) copy-start(bf16[1,512,1,1,512]{4,2,3,0,1:T(2,128)(2,1)} %copy.56) | copy-start | bytes 1572868
  677.5 3.6 copy-start.15
  677.5 3.6 copy-start.17
  677.5 3.6 copy-start.23
  677.5 3.6 copy-start.27
  691.6 316.1 %reduce-scatter.14.cloned.1.call-start = ((), (), s32[]{:S(2)}) async-start(), calls=%async_computation.18 | async-start | bytes 17825792 | tf_op jit(solution)/shard_map/reduce_scatter | solution.py:230
  710.2 478.1 %reduce-scatter.12.cloned.1.call-start = ((), (), s32[]{:S(2)}) async-start(), calls=%async_computation.17 | async-start | bytes 17825792 | tf_op jit(solution)/shard_map/reduce_scatter | solution.py:228
  725.9 1.9 copy-start.13
  725.9 2.4 copy-start.21
  725.9 600.6 %reduce-scatter.6.cloned.1.call-start = ((), (), s32[]{:S(2)}) async-start(), calls=%async_computation.14 | async-start | bytes 13369344 | tf_op jit(solution)/shard_map/reduce_scatter | solution.py:216
  789.9 8.5 copy-start.4
  789.9 8.5 copy-start.11
  789.9 8.5 copy-start.12
  789.9 8.5 copy-start.19
  798.0 2.7 copy-start.20
  798.0 2.7 copy-start.28
  818.2 595.9 %all-reduce.13.cloned.1.call-start = ((), (), s32[]{:S(2)}) async-start(), calls=%async_computation.19 | async-start | bytes 6291456 | tf_op jit(solution)/shard_map/psum | solution.py:234
  (3 other events, 3.0 us)
Sparse Core Ops, SparseCore 0:
  10.3 103.2 all-gather.8
  115.9 59.6 all-gather.10
  177.7 40.1 all-gather.12
  219.9 73.0 all-gather.14
  295.0 73.1 all-gather.16
  418.5 72.8 reduce-scatter.9
  691.7 135.2 reduce-scatter.7
  831.1 176.5 reduce-scatter.13
  1011.9 176.4 reduce-scatter.11
  1192.2 134.2 reduce-scatter.5
  1328.9 85.0 all-reduce.12
where the time goes:
time: 1440 us; the launch traced here: 1430 us
  waiting for transfers between devices  647 us (45%)
  matrix products  326 us (23%)
  blocking collectives  313 us (22%)
  local copies, waits for them, and re-layouts  73.4 us (5%)
  other arithmetic  42.9 us (3%)
  between operations  17.8 us (1%)
    reduce_scatter x1, waiting for transfers between devices, on_device(): lax.psum_scatter(grad_fc2, 'fsdp', scatter_dimension=0, tiled=True)  181 us
    reduce_scatter x1, waiting for transfers between devices, on_device(): lax.psum_scatter(grad_fc1, 'fsdp', scatter_dimension=0, tiled=True)  181 us
    unnamed x3, blocking collectives  153 us
    psum x1, waiting for transfers between devices, on_device(): lax.psum((shard_qkv, shard_bqv, shard_proj, shard_bproj, shard_fc1, shard...  85.2 us
    dot_general x2, matrix products, attend_backward(): jnp.einsum('bhqk,bkhd->bqhd', d_raw, keys_all, preferred_element_type=jnp...  73.6 us
    reduce_scatter x1, waiting for transfers between devices, on_device(): lax.psum_scatter(grad_ada.astype(jnp.bfloat16), 'fsdp', scatter_dimension...  67 us
    dot_general x2, matrix products, attend_backward(): jnp.einsum('bhqk,bqhd->bkhd', d_raw, q_block, preferred_element_type=jnp....  62.2 us
    all_gather x1, waiting for transfers between devices, on_device(): lax.all_gather(w_ada, 'fsdp', axis=0, tiled=True)  56.9 us
  transfers between devices with their start and end apart: 13, of which 8 were waited for; matrix products, arithmetic and copies ran while one was open for 27% of the time, Pallas kernels for 0%

commit v1 on v0

--- a/solution.py
+++ b/solution.py
@@ -7,6 +7,27 @@
 HD = 64
 norm_eps = 1e-06
 block_rows = 512
+
+
+def ring_gather(x, axis, dim):
+    size, index, rows = (lax.axis_size(axis), lax.axis_index(axis), x.shape[dim])
+    upward = [(i, (i + 1) % size) for i in range(size)]
+    downward = [(i, (i - 1) % size) for i in range(size)]
+    whole = jnp.zeros((*x.shape[:dim], size * rows, *x.shape[dim + 1 :]), x.dtype)
+    whole = lax.dynamic_update_slice_in_dim(whole, x, index * rows, axis=dim)
+    from_left = from_right = x
+    half = size // 2
+    for hop in range(1, half + 1):
+        from_left = lax.ppermute(from_left, axis, upward)
+        whole = lax.dynamic_update_slice_in_dim(
+            whole, from_left, (index - hop) % size * rows, axis=dim
+        )
+        if hop < size - half:
+            from_right = lax.ppermute(from_right, axis, downward)
+            whole = lax.dynamic_update_slice_in_dim(
+                whole, from_right, (index + hop) % size * rows, axis=dim
+            )
+    return whole
 
 
 def layer_norm(values):
@@ -101,7 +122,7 @@
     group_width = model_width // groups
     per_group = group_width // head_dim
     ada_w, ada_b, qkv_w, qv_b, proj_w, proj_b, fc1_w, fc1_b, fc2_w, fc2_b = (
-        lax.all_gather(w_ada, "fsdp", axis=0, tiled=True),
+        ring_gather(w_ada, "fsdp", 0),
         lax.all_gather(b_ada, "fsdp", axis=0, tiled=True),
         lax.all_gather(w_qkv, "fsdp", axis=0, tiled=True),
         lax.all_gather(b_qv, "fsdp", axis=0, tiled=True),

time: 1440 us -> 1500 us (1.042)
  starting transfers between devices: 8.89 us -> 115 us
  waiting for transfers between devices: 647 us -> 574 us
  local copies, waits for them, and re-layouts: 73.4 us -> 94.4 us
    ppermute x0 -> x15, starting transfers between devices: none -> 107 us  [the longest x8 89.3 us: ring_gather(): from_left = lax.ppermute(from_left, axis, upward)]
    all_gather x1 -> x0, waiting for transfers between devices: 56.9 us -> none  [on_device(): lax.all_gather(w_ada, 'fsdp', axis=0, tiled=True)]
    all_gather x1, waiting for transfers between devices: 55.6 us -> 0.02 us  [on_device(): lax.all_gather(w_qkv, 'fsdp', axis=0, tiled=True)]
    ppermute x0 -> x15, waiting for transfers between devices: none -> 40.4 us  [the longest x8 26.1 us: ring_gather(): from_left = lax.ppermute(from_left, axis, upward)]
    dynamic_update_slice x0 -> x16, local copies, waits for them, and re-layouts: none -> 15.3 us  [the longest x8 7.69 us: ring_gather(): lax.dynamic_update_slice_in_dim(whole, from_left, (index - hop) % size *...]
  transfers between devices with their start and end apart: 13 -> 27, of which waited for: 8 -> 12; matrix products, arithmetic and copies ran while one was open for 27% -> 27% of each run, Pallas kernels for 0% -> 0%
where the time goes in v1:
time: 1500 us; the launch traced here: 1490 us
  waiting for transfers between devices  574 us (38%)
  matrix products  325 us (22%)
  blocking collectives  318 us (21%)
  starting transfers between devices  115 us (8%)
  local copies, waits for them, and re-layouts  94.4 us (6%)
  other arithmetic  42.6 us (3%)
  between operations  18.5 us (1%)
    reduce_scatter x1, waiting for transfers between devices, on_device(): lax.psum_scatter(grad_fc2, 'fsdp', scatter_dimension=0, tiled=True)  181 us
    reduce_scatter x1, waiting for transfers between devices, on_device(): lax.psum_scatter(grad_fc1, 'fsdp', scatter_dimension=0, tiled=True)  181 us
    unnamed x3, blocking collectives  153 us
    ppermute x8, starting transfers between devices, ring_gather(): from_left = lax.ppermute(from_left, axis, upward)  89.3 us
    psum x1, waiting for transfers between devices, on_device(): lax.psum((shard_qkv, shard_bqv, shard_proj, shard_bproj, shard_fc1, shard...  85.1 us
    dot_general x2, matrix products, attend_backward(): jnp.einsum('bhqk,bkhd->bqhd', d_raw, keys_all, preferred_element_type=jnp...  73.7 us
    reduce_scatter x1, waiting for transfers between devices, on_device(): lax.psum_scatter(grad_ada.astype(jnp.bfloat16), 'fsdp', scatter_dimension...  67.1 us
    dot_general x2, matrix products, attend_backward(): jnp.einsum('bhqk,bqhd->bkhd', d_raw, q_block, preferred_element_type=jnp....  62.2 us
  transfers between devices with their start and end apart: 27, of which 12 were waited for; matrix products, arithmetic and copies ran while one was open for 27% of the time, Pallas kernels for 0%

profile of v1, /device:TPU:0, one launch (start us, length us, event | category | flops | bytes accessed | tf_op | source)
XLA Modules:
  0.0 1487.1 jit_solution(2591025881636995042)
XLA Ops:
  19.1 28.6 %all-gather.1 = bf16[16,1,128]{2,1,0:T(2,128)(2,1)S(1)} all-gather(bf16[1,1,128]{2,1,0:T(2,128)(2,1)} %bitcast.251), channel_id=1, replica_groups=mesh['fsdp'=16,'seq'=2] {'fsdp'}, dimensions={0}, use_global_device_ids=true | all-gather | bytes 4352 | tf_op jit(solution)/shard_map/all_gather | solution.py:128
  47.7 19.1 %all-gather = bf16[16,1,384]{2,1,0:T(2,128)(2,1)S(1)} all-gather(bf16[1,1,384]{2,1,0:T(2,128)(2,1)S(1)} %reshape.506), channel_id=1, replica_groups=mesh['fsdp'=16,'seq'=2] {'fsdp'}, dimensions={0}, use_global_device_ids=true | all-gather | bytes 13056 | tf_op jit(solution)/shard_map/all_gather | solution.py:126
  76.8 7.6 collective-permute-done.3
  89.0 14.3 collective-permute-start.4
  107.1 20.2 %collective-permute-start.6 = (bf16[64,6144]{1,0:T(8,128)(2,1)S(1)}, bf16[64,6144]{1,0:T(8,128)(2,1)S(1)}, u32[]{:S(2)}, u32[]{:S(2)}) collective-permute-start(bf16[64,6144]{1,0:T(8,128)(2,1)S(1)} %collective-permute-done.4), channel_id=1, source_target_pairs={{0,2},{2,4},{4,6},{6,8},{8,10},{10,12},{12,14},{14,16},{16,18},{18... | collective-permute-start | bytes 2359304 | tf_op jit(solution)/shard_map/ppermute | solution.py:21
  129.2 17.6 %collective-permute-start.8 = (bf16[64,6144]{1,0:T(8,128)(2,1)S(1)}, bf16[64,6144]{1,0:T(8,128)(2,1)S(1)}, u32[]{:S(2)}, u32[]{:S(2)}) collective-permute-start(bf16[64,6144]{1,0:T(8,128)(2,1)S(1)} %collective-permute-done.6), channel_id=1, source_target_pairs={{0,2},{2,4},{4,6},{6,8},{8,10},{10,12},{12,14},{14,16},{16,18},{18... | collective-permute-start | bytes 2359304 | tf_op jit(solution)/shard_map/ppermute | solution.py:21
  148.7 15.1 %collective-permute-start.10 = (bf16[64,6144]{1,0:T(8,128)(2,1)S(1)}, bf16[64,6144]{1,0:T(8,128)(2,1)S(1)}, u32[]{:S(2)}, u32[]{:S(2)}) collective-permute-start(bf16[64,6144]{1,0:T(8,128)(2,1)S(1)} %collective-permute-done.8), channel_id=1, source_target_pairs={{0,2},{2,4},{4,6},{6,8},{8,10},{10,12},{12,14},{14,16},{16,18},{18... | collective-permute-start | bytes 2359304 | tf_op jit(solution)/shard_map/ppermute | solution.py:21
  165.7 6.7 collective-permute-done.11
  178.6 11.9 collective-permute-start.12
  192.4 17.0 %collective-permute-done.12 = bf16[64,6144]{1,0:T(8,128)(2,1)S(1)} collective-permute-done((bf16[64,6144]{1,0:T(8,128)(2,1)S(1)}, bf16[64,6144]{1,0:T(8,128)(2,1)S(1)}, u32[]{:S(2)}, u32[]{:S(2)}) %collective-permute-start.12) | collective-permute-done | bytes 786464 | tf_op jit(solution)/shard_map/ppermute | solution.py:21
  209.4 10.3 collective-permute-start.14
  221.6 7.4 collective-permute-done.14
  237.1 7.9 add_convert_fusion
  245.1 7.1 reshape.484
  252.7 39.6 %all_to_all.63 = bf16[1,512,3,2,512]{4,1,2,0,3:T(8,128)(2,1)S(1)} all-to-all(bf16[1,512,3,2,512]{4,1,2,0,3:T(8,128)(2,1)S(1)} %copy.46), channel_id=1, replica_groups=mesh['fsdp'=16,'seq'=2] {'seq'}, dimensions={3} | all-to-all | bytes 6291456 | tf_op jit(solution)/shard_map/all_to_all | solution.py:153
  298.9 8.6 multiply_reduce_fusion.3
  324.0 7.7 fusion.72
  336.5 9.0 reduce.38
  354.4 30.8 %all-reduce.10 = (bf16[1024]{0:T(1024)(128)(2,1)S(1)}, bf16[1024]{0:T(1024)(128)(2,1)S(1)}) all-reduce(bf16[1024]{0:T(1024)(128)(2,1)S(1)} %dynamic-update-slice, bf16[1024]{0:T(1024)(128)(2,1)S(1)} %dynamic-update-slice.1), channel_id=1, replica_groups=mesh['fsdp'=16,'seq'=2] {'fsdp'}, use_global_device_ids=true, to_apply=%add | all-reduce | flops 2048 | bytes 8192
  385.2 17.2 %all-gather.2 = bf16[16,1,256]{2,1,0:T(2,128)(2,1)S(1)} all-gather(bf16[1,1,256]{2,1,0:T(2,128)(2,1)S(1)} %reshape.510), channel_id=1, replica_groups=mesh['fsdp'=16,'seq'=2] {'fsdp'}, dimensions={0}, use_global_device_ids=true | all-gather | bytes 8704 | tf_op jit(solution)/shard_map/all_gather | solution.py:132
  416.9 12.0 fusion.122
  428.9 14.3 convert_reduce_fusion
  449.4 12.6 convert_reduce_fusion.3
  476.9 9.3 all-to-all-done.2
  490.2 8.1 fusion.29
  498.4 8.7 add_convert_fusion.1
  513.0 8.1 fusion.90
  521.1 37.1 %fusion.64 = bf16[8,64,512]{2,1,0:T(8,128)(2,1)} fusion(bf16[1024,8,64]{0,2,1:T(8,128)(2,1)S(1)} %bitcast.199, f32[8,512,1024]{2,1,0:T(8,128)} %fusion.90, f32[8,512]{1,0:T(8,128)S(1)} %log_add_fusion, f32[8,512,1024]{2,1,0:T(8,128)} %copy-done), kind=kOutput, calls=%fused_computation.90 | convolution fusion | flops 574886912 | bytes 35143680 | tf_op jit(solution)/shard_map/bhqk,bkhd->bqhd/dot_general | solution.py:95
  561.7 8.1 fusion.89
  569.8 36.6 %fusion.67 = bf16[8,64,512]{2,1,0:T(8,128)(2,1)S(1)} fusion(bf16[1024,8,64]{0,2,1:T(8,128)(2,1)S(1)} %bitcast.200, f32[8,512,1024]{2,1,0:T(8,128)} %fusion.89, f32[8,512]{1,0:T(8,128)S(1)} %log_add_fusion.1, f32[8,512,1024]{2,1,0:T(8,128)} %get-tuple-element.67), kind=kOutput, calls=%fused_computation.91 | convolution fusion | flops 574886912 | bytes 35143680 | tf_op jit(solution)/shard_map/bhqk,bkhd->bqhd/dot_general | solution.py:95
  608.5 30.7 %fusion.11 = f32[8,64,1024]{2,1,0:T(8,128)} fusion(f32[8,512,1024]{2,1,0:T(8,128)} %fusion.89, f32[8,512,1024]{2,1,0:T(8,128)} %get-tuple-element.67, f32[8,512]{1,0:T(8,128)S(1)} %log_add_fusion.1, bf16[1,1024,8,64]{1,3,2,0:T(8,128)(2,1)S(1)} %bitcast.210), kind=kOutput, calls=%fused_computation.21 | convolution fusion | flops 574624768 | bytes 69763072 | tf_op jit(solution)/shard_map/bhqk,bqhd->bkhd/dot_general | solution.py:97
  639.2 31.5 %add_convert_fusion.2 = bf16[8,64,1024]{2,1,0:T(8,128)(2,1)} fusion(f32[8,64,1024]{2,1,0:T(8,128)} %fusion.11, f32[8,512,1024]{2,1,0:T(8,128)} %fusion.90, f32[8,512]{1,0:T(8,128)S(1)} %log_add_fusion, f32[8,512,1024]{2,1,0:T(8,128)} %copy-done, bf16[1,1024,8,64]{1,3,2,0:T(8,128)(2,1)} %bitcast.208), kind=kOutput, calls=%fused_computation.82 | convolution fusion | flops 575673344 | bytes 70811648 | tf_op jit(solution)/shard_map/bhqk,bqhd->bkhd/dot_general | solution.py:97
  676.6 8.6 pad_maximum_fusion
  685.2 50.4 %all_to_all.64 = bf16[1,1024,3,1,512]{4,2,3,0,1:T(4,128)(2,1)S(1)} all-to-all(bf16[1,1024,3,1,512]{4,2,3,0,1:T(4,128)(2,1)S(1)} %pad_maximum_fusion), channel_id=1, replica_groups=mesh['fsdp'=16,'seq'=2] {'seq'}, dimensions={1} | all-to-all | bytes 6291456 | tf_op jit(solution)/shard_map/all_to_all | solution.py:218
  739.3 10.5 fusion.117
  749.9 18.8 %fusion.79 = f32[4096,1024]{1,0:T(8,128)} fusion(bf16[1,512,1024]{2,1,0:T(8,128)(2,1)} %param.25, f32[1024]{0:T(1024)S(1)} %bitcast.243, f32[512,4096]{1,0:T(8,128)} %fusion.122, f32[4096]{0:T(1024)S(1)} %bitcast.236), kind=kOutput, calls=%fused_computation.102 | convolution fusion | flops 4317511680 | bytes 26234880 | tf_op jit(solution)/shard_map/btf,btd->fd/dot_general | solution.py:189
  769.4 14.9 %fusion.120 = f32[1024,4096]{1,0:T(8,128)} fusion(bf16[512,4096]{1,0:T(8,128)(2,1)} %copy-done.39, f32[1,512,1024]{2,1,0:T(8,128)} %copy-done.9, f32[1024]{0:T(1024)S(1)} %bitcast.240, f32[1024]{0:T(1024)S(1)} %bitcast.230, f32[512]{0:T(512)S(1)} %add_rsqrt_fusion, f32[512]{0:T(512)S(1)} %broadcast_multiply_fusion.4), kind=kOutput, calls=%fused_computation.181 | convolution fusion | flops 4297588736 | bytes 23080960 | tf_op jit(solution)/shard_map/btd,btf->df/dot_general | solution.py:193
  786.7 61.4 %all-reduce.7 = (f32[2048]{0:T(1024)S(1)}, f32[1024]{0:T(1024)S(1)}, f32[4096]{0:T(1024)S(1)}, f32[1024]{0:T(1024)S(1)}) all-reduce(f32[2048]{0:T(1024)S(1)} %pad_maximum_fusion.2, f32[1024]{0:T(1024)S(1)} %get-tuple-element.47, f32[4096]{0:T(1024)S(1)} %copy-done.23, ...), channel_id=5, replica_groups=mesh['fsdp'=16,'seq'=2] {'fsdp'}, use_global_device_ids=true, to_apply=%region_26.27.clone | all-reduce | flops 8192 | bytes 65536
  848.4 8.1 fusion.51
  859.2 9.5 all-reduce.8
  868.8 7.4 multiply_convert_fusion
  876.3 8.4 reduce-scatter.8.cloned.1.call-done
  884.7 180.7 %reduce-scatter.14.cloned.1.call-done = f32[256,1024]{1,0:T(8,128)} async-done(((f32[4096,1024]{1,0:T(8,128)}), f32[256,1024]{1,0:T(8,128)}) %reduce-scatter.14.cloned.1.call-update) | async-done | bytes 1048592 | tf_op jit(solution)/shard_map/reduce_scatter | solution.py:251
  1065.4 180.6 %reduce-scatter.12.cloned.1.call-done = f32[64,4096]{1,0:T(8,128)} async-done(((f32[1024,4096]{1,0:T(8,128)}), f32[64,4096]{1,0:T(8,128)}) %reduce-scatter.12.cloned.1.call-update) | async-done | bytes 1048592 | tf_op jit(solution)/shard_map/reduce_scatter | solution.py:249
  1246.6 61.3 %all-reduce.2 = bf16[6144]{0:T(1024)(128)(2,1)S(1)} all-reduce(bf16[6144]{0:T(1024)(128)(2,1)S(1)} %convert_reduce_fusion.5), channel_id=3, replica_groups=mesh['fsdp'=16,'seq'=2] {'fsdp'}, use_global_device_ids=true, to_apply=%region_22.23.clone | all-reduce | flops 6144 | bytes 24576
  1308.6 8.7 fusion.95
  1317.2 67.1 %reduce-scatter.6.cloned.1.call-done = bf16[64,6144]{1,0:T(8,128)(2,1)} async-done(((bf16[1024,6144]{1,0:T(8,128)(2,1)}), bf16[64,6144]{1,0:T(8,128)(2,1)}) %reduce-scatter.6.cloned.1.call-update) | async-done | bytes 786448 | tf_op jit(solution)/shard_map/reduce_scatter | solution.py:237
  1386.7 85.1 %all-reduce.13.cloned.1.call-done = (f32[64,3072]{1,0:T(8,128)}, f32[64,1024]{1,0:T(8,128)}, f32[64,4096]{1,0:T(8,128)}, f32[256,1024]{1,0:T(8,128)}) async-done(((f32[64,3072]{1,0:T(8,128)}, f32[64,1024]{1,0:T(8,128)}, f32[64,4096]{1,0:T(8,128)}, f32[256,1024]{1,0:T(8,128)}), (f32[64,3072]{1,0:T(8,128)}, f32[64,1024]{1,0:T(8,128)}, f32[64,4096]{1,0:T(8,128)}, ...) | async-done | bytes 3145744 | tf_op jit(solution)/shard_map/psum | solution.py:255
  (235 shorter events, 166.6 us)
Async XLA Ops:
  7.2 65.9 %copy-start.13 = (bf16[64,6144]{1,0:T(8,128)(2,1)S(1)}, bf16[64,6144]{1,0:T(8,128)(2,1)}, u32[]{:S(2)}) copy-start(bf16[64,6144]{1,0:T(8,128)(2,1)} %param.15) | copy-start | bytes 2359300
  7.2 229.4 %all-gather.8.cloned.1.call-start = ((), (), s32[]{:S(2)}) async-start(), calls=%async_computation.9 | async-start | bytes 6684672 | tf_op jit(solution)/shard_map/all_gather | solution.py:127
  7.9 402.7 %all-gather.10.cloned.1.call-start = ((), (), s32[]{:S(2)}) async-start(), calls=%async_computation.10 | async-start | bytes 2228224 | tf_op jit(solution)/shard_map/all_gather | solution.py:129
  8.7 408.2 %all-gather.12.cloned.1.call-start = ((), (), s32[]{:S(2)}) async-start(), calls=%async_computation.11 | async-start | bytes 8912896 | tf_op jit(solution)/shard_map/all_gather | solution.py:131
  9.4 419.5 %all-gather.14.cloned.1.call-start = ((), (), s32[]{:S(2)}) async-start(), calls=%async_computation.12 | async-start | bytes 8912896 | tf_op jit(solution)/shard_map/all_gather | solution.py:133
  9.5 64.5 %collective-permute-start.1 = (bf16[64,6144]{1,0:T(8,128)(2,1)}, bf16[64,6144]{1,0:T(8,128)(2,1)S(1)}, u32[]{:S(2)}, u32[]{:S(2)}) collective-permute-start(bf16[64,6144]{1,0:T(8,128)(2,1)} %param.15), channel_id=1, source_target_pairs={{0,30},{2,0},{4,2},{6,4},{8,6},{10,8},{12,10},{14,12},{16,14},{18,... | collective-permute-start | bytes 2359304 | tf_op jit(solution)/shard_map/ppermute | solution.py:26
  15.0 59.8 %collective-permute-start = (bf16[64,6144]{1,0:T(8,128)(2,1)}, bf16[64,6144]{1,0:T(8,128)(2,1)S(1)}, u32[]{:S(2)}, u32[]{:S(2)}) collective-permute-start(bf16[64,6144]{1,0:T(8,128)(2,1)} %param.15), channel_id=1, source_target_pairs={{0,2},{2,4},{4,6},{6,8},{8,10},{10,12},{12,14},{14,16},{16,18},{18... | collective-permute-start | bytes 2359304 | tf_op jit(solution)/shard_map/ppermute | solution.py:21
  17.4 219.2 %copy-start.18 = (f32[512]{0:T(512)}, f32[512]{0:T(512)S(1)}, u32[]{:S(2)}) copy-start(f32[512]{0:T(512)S(1)} %broadcast_multiply_fusion.5) | copy-start | bytes 6148
  19.1 217.5 %copy-start.24 = (f32[512]{0:T(512)}, f32[512]{0:T(512)S(1)}, u32[]{:S(2)}) copy-start(f32[512]{0:T(512)S(1)} %add_rsqrt_fusion.1) | copy-start | bytes 6148
  74.0 10.3 collective-permute-start.3
  74.8 14.2 collective-permute-start.2
  84.3 20.9 %collective-permute-start.5 = (bf16[64,6144]{1,0:T(8,128)(2,1)S(1)}, bf16[64,6144]{1,0:T(8,128)(2,1)S(1)}, u32[]{:S(2)}, u32[]{:S(2)}) collective-permute-start(bf16[64,6144]{1,0:T(8,128)(2,1)S(1)} %collective-permute-done.3), channel_id=1, source_target_pairs={{0,30},{2,0},{4,2},{6,4},{8,6},{10,8},{12,10},{14,12},{16,14},{18,... | collective-permute-start | bytes 2359304 | tf_op jit(solution)/shard_map/ppermute | solution.py:26
  89.0 18.1 %collective-permute-start.4 = (bf16[64,6144]{1,0:T(8,128)(2,1)S(1)}, bf16[64,6144]{1,0:T(8,128)(2,1)S(1)}, u32[]{:S(2)}, u32[]{:S(2)}) collective-permute-start(bf16[64,6144]{1,0:T(8,128)(2,1)S(1)} %collective-permute-done.2), channel_id=1, source_target_pairs={{0,2},{2,4},{4,6},{6,8},{8,10},{10,12},{12,14},{14,16},{16,18},{18... | collective-permute-start | bytes 2359304 | tf_op jit(solution)/shard_map/ppermute | solution.py:21
  105.2 124.8 %copy-start.14 = (bf16[1,1024]{1,0:T(2,128)(2,1)S(1)}, bf16[1,1024]{1,0:T(2,128)(2,1)}, u32[]{:S(2)}) copy-start(bf16[1,1024]{1,0:T(2,128)(2,1)} %param.14) | copy-start | bytes 6148
  105.2 24.0 %collective-permute-start.7 = (bf16[64,6144]{1,0:T(8,128)(2,1)S(1)}, bf16[64,6144]{1,0:T(8,128)(2,1)S(1)}, u32[]{:S(2)}, u32[]{:S(2)}) collective-permute-start(bf16[64,6144]{1,0:T(8,128)(2,1)S(1)} %collective-permute-done.5), channel_id=1, source_target_pairs={{0,30},{2,0},{4,2},{6,4},{8,6},{10,8},{12,10},{14,12},{16,14},{18,... | collective-permute-start | bytes 2359304 | tf_op jit(solution)/shard_map/ppermute | solution.py:26
  107.1 22.1 %collective-permute-start.6 = (bf16[64,6144]{1,0:T(8,128)(2,1)S(1)}, bf16[64,6144]{1,0:T(8,128)(2,1)S(1)}, u32[]{:S(2)}, u32[]{:S(2)}) collective-permute-start(bf16[64,6144]{1,0:T(8,128)(2,1)S(1)} %collective-permute-done.4), channel_id=1, source_target_pairs={{0,2},{2,4},{4,6},{6,8},{8,10},{10,12},{12,14},{14,16},{16,18},{18... | collective-permute-start | bytes 2359304 | tf_op jit(solution)/shard_map/ppermute | solution.py:21
  129.2 19.4 %collective-permute-start.9 = (bf16[64,6144]{1,0:T(8,128)(2,1)S(1)}, bf16[64,6144]{1,0:T(8,128)(2,1)S(1)}, u32[]{:S(2)}, u32[]{:S(2)}) collective-permute-start(bf16[64,6144]{1,0:T(8,128)(2,1)S(1)} %collective-permute-done.7), channel_id=1, source_target_pairs={{0,30},{2,0},{4,2},{6,4},{8,6},{10,8},{12,10},{14,12},{16,14},{18,... | collective-permute-start | bytes 2359304 | tf_op jit(solution)/shard_map/ppermute | solution.py:26
  129.2 19.5 %collective-permute-start.8 = (bf16[64,6144]{1,0:T(8,128)(2,1)S(1)}, bf16[64,6144]{1,0:T(8,128)(2,1)S(1)}, u32[]{:S(2)}, u32[]{:S(2)}) collective-permute-start(bf16[64,6144]{1,0:T(8,128)(2,1)S(1)} %collective-permute-done.6), channel_id=1, source_target_pairs={{0,2},{2,4},{4,6},{6,8},{8,10},{10,12},{12,14},{14,16},{16,18},{18... | collective-permute-start | bytes 2359304 | tf_op jit(solution)/shard_map/ppermute | solution.py:21
  148.6 23.9 %collective-permute-start.11 = (bf16[64,6144]{1,0:T(8,128)(2,1)S(1)}, bf16[64,6144]{1,0:T(8,128)(2,1)S(1)}, u32[]{:S(2)}, u32[]{:S(2)}) collective-permute-start(bf16[64,6144]{1,0:T(8,128)(2,1)S(1)} %collective-permute-done.9), channel_id=1, source_target_pairs={{0,30},{2,0},{4,2},{6,4},{8,6},{10,8},{12,10},{14,12},{16,14},{18,... | collective-permute-start | bytes 2359304 | tf_op jit(solution)/shard_map/ppermute | solution.py:26
  148.7 29.9 %collective-permute-start.10 = (bf16[64,6144]{1,0:T(8,128)(2,1)S(1)}, bf16[64,6144]{1,0:T(8,128)(2,1)S(1)}, u32[]{:S(2)}, u32[]{:S(2)}) collective-permute-start(bf16[64,6144]{1,0:T(8,128)(2,1)S(1)} %collective-permute-done.8), channel_id=1, source_target_pairs={{0,2},{2,4},{4,6},{6,8},{8,10},{10,12},{12,14},{14,16},{16,18},{18... | collective-permute-start | bytes 2359304 | tf_op jit(solution)/shard_map/ppermute | solution.py:21
  172.5 48.1 %collective-permute-start.13 = (bf16[64,6144]{1,0:T(8,128)(2,1)S(1)}, bf16[64,6144]{1,0:T(8,128)(2,1)S(1)}, u32[]{:S(2)}, u32[]{:S(2)}) collective-permute-start(bf16[64,6144]{1,0:T(8,128)(2,1)S(1)} %collective-permute-done.11), channel_id=1, source_target_pairs={{0,30},{2,0},{4,2},{6,4},{8,6},{10,8},{12,10},{14,12},{16,14},{18,... | collective-permute-start | bytes 2359304 | tf_op jit(solution)/shard_map/ppermute | solution.py:26
  178.6 30.8 %collective-permute-start.12 = (bf16[64,6144]{1,0:T(8,128)(2,1)S(1)}, bf16[64,6144]{1,0:T(8,128)(2,1)S(1)}, u32[]{:S(2)}, u32[]{:S(2)}) collective-permute-start(bf16[64,6144]{1,0:T(8,128)(2,1)S(1)} %collective-permute-done.10), channel_id=1, source_target_pairs={{0,2},{2,4},{4,6},{6,8},{8,10},{10,12},{12,14},{14,16},{16,18},{18... | collective-permute-start | bytes 2359304 | tf_op jit(solution)/shard_map/ppermute | solution.py:21
  209.4 19.7 %collective-permute-start.14 = (bf16[64,6144]{1,0:T(8,128)(2,1)S(1)}, bf16[64,6144]{1,0:T(8,128)(2,1)S(1)}, u32[]{:S(2)}, u32[]{:S(2)}) collective-permute-start(bf16[64,6144]{1,0:T(8,128)(2,1)S(1)} %collective-permute-done.12), channel_id=1, source_target_pairs={{0,2},{2,4},{4,6},{6,8},{8,10},{10,12},{12,14},{14,16},{16,18},{18... | collective-permute-start | bytes 2359304 | tf_op jit(solution)/shard_map/ppermute | solution.py:21
  236.5 8.5 copy-start.28
  236.6 180.4 %copy-start.26 = (f32[1,1,1024]{2,1,0:T(1,128)}, f32[1,1,1024]{2,1,0:T(1,128)S(1)}, u32[]{:S(2)}) copy-start(f32[1,1,1024]{2,1,0:T(1,128)S(1)} %get-tuple-element.53) | copy-start | bytes 12292
  298.9 20.8 %copy-start = (f32[8,512,1024]{2,1,0:T(8,128)}, f32[8,512,1024]{2,1,0:T(8,128)S(1)}, u32[]{:S(2)}) copy-start(f32[8,512,1024]{2,1,0:T(8,128)S(1)} %get-tuple-element.65) | copy-start | bytes 50331652
  307.5 8.6 copy-start.1
  331.7 20.9 %copy-start.35 = (bf16[256]{0:T(256)(128)(2,1)S(1)}, bf16[256]{0:T(256)(128)(2,1)}, u32[]{:S(2)}) copy-start(bf16[256]{0:T(256)(128)(2,1)} %param.22) | copy-start | bytes 1540
  331.7 20.9 %copy-start.31 = (u32[32]{0:T(128)S(1)}, u32[32]{0:T(128)}, u32[]{:S(2)}) copy-start(u32[32]{0:T(128)} %constant.152) | copy-start | bytes 388
  331.7 22.2 %copy-start.36 = (bf16[64]{0:T(256)(128)(2,1)S(1)}, bf16[64]{0:T(256)(128)(2,1)}, u32[]{:S(2)}) copy-start(bf16[64]{0:T(256)(128)(2,1)} %param.24) | copy-start | bytes 388
  331.8 22.4 %copy-start.37 = (bf16[64]{0:T(256)(128)(2,1)S(1)}, bf16[64]{0:T(256)(128)(2,1)}, u32[]{:S(2)}) copy-start(bf16[64]{0:T(256)(128)(2,1)} %param.20) | copy-start | bytes 388
  335.9 74.7 %copy-start.3 = (bf16[1,512,1024]{2,1,0:T(8,128)(2,1)S(1)}, bf16[1,512,1024]{2,1,0:T(8,128)(2,1)}, u32[]{:S(2)}) copy-start(bf16[1,512,1024]{2,1,0:T(8,128)(2,1)} %param.13) | copy-start | bytes 3145732
  348.1 54.3 %all-to-all-start.1 = ((bf16[2,2,131072]{2,1,0:T(2,128)(2,1)}), bf16[2,2,131072]{2,1,0:T(2,128)(2,1)}, u32[]{:S(2)}, u32[]{:S(2)}) async-start(bf16[2,2,131072]{2,1,0:T(2,128)(2,1)} %reshape.533), calls=%async_computation.1 | async-start | bytes 2097152 | tf_op jit(solution)/shard_map/all_to_all | solution.py:165
  385.2 30.1 %copy-start.20 = (f32[1024]{0:T(1024)}, f32[1024]{0:T(1024)S(1)}, u32[]{:S(2)}) copy-start(f32[1024]{0:T(1024)S(1)} %convert_element_type.179) | copy-start | bytes 12292
  416.9 12.0 copy-start.34
  428.9 14.3 copy-start.10
  428.9 14.3 copy-start.32
  449.4 13.6 copy-start.33
  468.2 18.0 %all-to-all-start.2 = ((bf16[1,512,2,512]{3,1,0,2:T(8,128)(2,1)}), bf16[1,512,2,512]{3,1,0,2:T(8,128)(2,1)S(1)}, u32[]{:S(2)}, u32[]{:S(2)}) async-start(bf16[1,512,2,512]{3,1,0,2:T(8,128)(2,1)} %copy.53), calls=%async_computation.2 | async-start | bytes 2097152 | tf_op jit(solution)/shard_map/all_to_all | solution.py:206
  471.8 404.5 %reduce-scatter.10.cloned.1.call-start = ((), (), s32[]{:S(2)}) async-start(), calls=%async_computation.15 | async-start | bytes 4456448 | tf_op jit(solution)/shard_map/reduce_scatter | solution.py:247
  476.8 407.9 %reduce-scatter.8.cloned.1.call-start = ((), (), s32[]{:S(2)}) async-start(), calls=%async_computation.14 | async-start | bytes 13369344 | tf_op jit(solution)/shard_map/reduce_scatter | solution.py:245
  569.8 38.7 %copy-start.8 = (bf16[1,1024,1,1,512]{1,4,3,2,0:T(8,128)(2,1)S(1)}, bf16[1,1024,1,1,512]{1,4,3,2,0:T(8,128)(2,1)}, u32[]{:S(2)}) copy-start(bf16[1,1024,1,1,512]{1,4,3,2,0:T(8,128)(2,1)} %copy.49) | copy-start | bytes 3145732
  639.2 37.5 %copy-start.5 = (bf16[1,1024,1,1,512]{4,2,3,0,1:T(2,128)(2,1)S(1)}, bf16[1,1024,1,1,512]{4,2,3,0,1:T(2,128)(2,1)}, u32[]{:S(2)}) copy-start(bf16[1,1024,1,1,512]{4,2,3,0,1:T(2,128)(2,1)} %copy.58) | copy-start | bytes 3145732
  639.2 37.5 %copy-start.6 = (bf16[1,512,1,1,512]{4,2,3,0,1:T(2,128)(2,1)S(1)}, bf16[1,512,1,1,512]{4,2,3,0,1:T(2,128)(2,1)}, u32[]{:S(2)}) copy-start(bf16[1,512,1,1,512]{4,2,3,0,1:T(2,128)(2,1)} %copy.56) | copy-start | bytes 1572868
  749.8 315.6 %reduce-scatter.14.cloned.1.call-start = ((), (), s32[]{:S(2)}) async-start(), calls=%async_computation.17 | async-start | bytes 17825792 | tf_op jit(solution)/shard_map/reduce_scatter | solution.py:251
  768.7 477.3 %reduce-scatter.12.cloned.1.call-start = ((), (), s32[]{:S(2)}) async-start(), calls=%async_computation.16 | async-start | bytes 17825792 | tf_op jit(solution)/shard_map/reduce_scatter | solution.py:249
  784.3 600.0 %reduce-scatter.6.cloned.1.call-start = ((), (), s32[]{:S(2)}) async-start(), calls=%async_computation.13 | async-start | bytes 13369344 | tf_op jit(solution)/shard_map/reduce_scatter | solution.py:237
  876.2 595.5 %all-reduce.13.cloned.1.call-start = ((), (), s32[]{:S(2)}) async-start(), calls=%async_computation.18 | async-start | bytes 6291456 | tf_op jit(solution)/shard_map/psum | solution.py:255
  (19 other events, 77.9 us)
Sparse Core Ops, SparseCore 0:
  10.3 69.8 all-gather.7
  82.3 55.6 all-gather.9
  140.1 103.9 all-gather.11
  246.2 73.1 all-gather.13
  476.9 72.0 reduce-scatter.9
  749.9 134.6 reduce-scatter.7
  888.8 176.5 reduce-scatter.13
  1069.5 176.4 reduce-scatter.11
  1250.0 134.2 reduce-scatter.5
  1386.6 85.1 all-reduce.12
